TPU v7x, 32 devices: a whole 2x2x4 slice. The times are simulated.
32 devices in a mesh: dp: 16 (over z, y, core), tensor: 2 (over x).
Axes of the slice: x: 2, y: 2, z: 4, core: 2. Of those that a mesh axis runs over, the one named last changes fastest.
Arguments:
- tokens: float32 [16384, 1024], P(('dp', 'tensor')), may hold values from -6 to 6
- norm_gain: float32 [1024], P(('dp', 'tensor')), may hold values from 0.5 to 1.5
- w_z: bfloat16 [1024, 2048], P('dp', 'tensor'), may hold values from -0.1875 to 0.1875
- w_x: bfloat16 [1024, 2048], P('dp', 'tensor'), may hold values from -0.1875 to 0.1875
- w_dt: bfloat16 [1024, 32], P('dp', 'tensor'), may hold values from -0.1875 to 0.1875
- w_bc: bfloat16 [1024, 256], P(('dp', 'tensor')), may hold values from -0.1875 to 0.1875
- w_out: bfloat16 [1024, 2048], P('dp', 'tensor'), may hold values from -0.125 to 0.125
- conv_x_w: float32 [2048, 4], P('tensor'), may hold values from -3 to 3
- conv_x_b: float32 [2048], P('tensor'), may hold values from -0.5 to 0.5
- conv_bc_w: float32 [256, 4], P(('dp', 'tensor')), may hold values from -3 to 3
- conv_bc_b: float32 [256], P(('dp', 'tensor')), may hold values from -0.5 to 0.5
- a_log: float32 [32], P('tensor'), may hold values from -1 to 1.5
- d_skip: float32 [32], P('tensor'), may hold values from 0.5 to 1.5
- dt_bias: float32 [32], P('tensor'), may hold values from -7 to -2.5
- norm_w: float32 [2048], P('tensor'), may hold values from 0.5 to 1.5
- block_seq: int32 [64], P('dp'), may hold values from 0 to 63, as said below
- block_len: int32 [64], P('dp'), may hold values from 0 to 256, as said below
- cotangent: float32 [16384, 1024], P(('dp', 'tensor')), may hold values from -6 to 6
Outputs:
- output: float32 [16384, 1024], P(('dp', 'tensor'))
- d_tokens: float32 [16384, 1024], P(('dp', 'tensor'))
- d_gain: float32 [1024], P(('dp', 'tensor'))
- d_w_z: float32 [1024, 2048], P('dp', 'tensor')
- d_w_x: float32 [1024, 2048], P('dp', 'tensor')
- d_w_dt: float32 [1024, 32], P('dp', 'tensor')
- d_w_bc: float32 [1024, 256], P(('dp', 'tensor'))
- d_w_out: float32 [1024, 2048], P('dp', 'tensor')
- d_conv_x_w: float32 [2048, 4], P('tensor')
- d_conv_x_b: float32 [2048], P('tensor')
- d_conv_bc_w: float32 [256, 4], P(('dp', 'tensor'))
- d_conv_bc_b: float32 [256], P(('dp', 'tensor'))
- d_a_log: float32 [32], P('tensor')
- d_d_skip: float32 [32], P('tensor')
- d_dt_bias: float32 [32], P('tensor')
- d_norm_w: float32 [2048], P('tensor')
Inputs may be any that keep to these rules, and one draw needn't show every extreme that they name: `block_seq`: each index of dp holds 4 slots; a sequence takes consecutive slots of one index starting at a slot's first row, every slot but its last full; adjacent slots of one index carry the same value exactly when they hold one sequence; an empty slot has a value no other slot has. `block_len`: rows in use count from a slot's start; an empty slot has 0; fewer than 256 only in a sequence's last slot.
All inputs are finite; a program needn't handle non-finite values.
Results may differ from a plain program's by a relative error of at most 0.0082.
Values may be sent and summed in bfloat16 or wider, within the bound.
A program may use at most 192 MiB of HBM per device.

v0:
```python
import jax
import jax.numpy as jnp
from jax import lax
from jax.sharding import PartitionSpec as P

INNER = 2048
HEADDIM = 64
STATE = 128
BLOCK = 256


EPSILON = 1e-05
HIGHEST_PREC = lax.Precision.HIGHEST


def shift_rows(values, lag_rows):
    if lag_rows == 0:
        return values
    zero_rows = jnp.zeros((lag_rows,) + values.shape[1:], values.dtype)
    return jnp.concatenate([zero_rows, values[:-lag_rows]], axis=0)


def causal_conv(values, weights, bias_vec, keep_masks):
    taps_count = weights.shape[1]
    summed = jnp.zeros_like(values) + bias_vec[None, :]
    for offset in range(taps_count):
        lag_rows = taps_count - 1 - offset
        shifted = shift_rows(values, lag_rows) * keep_masks[lag_rows][:, None]
        summed = summed + shifted * weights[:, offset][None, :]
    return jax.nn.silu(summed)


def scan_heads(
    x_pre,
    bc_pre,
    dt_raw,
    conv_x_w,
    conv_x_b,
    conv_bc_w,
    conv_bc_b,
    a_log,
    d_skip,
    dt_bias,
    carry_flags,
    token_mask,
):
    row_count = x_pre.shape[0]
    slot_count = row_count // BLOCK
    head_count = dt_raw.shape[1]
    position = jnp.arange(row_count) % BLOCK
    carry_rows = jnp.repeat(carry_flags, BLOCK)
    keep_masks = [
        jnp.where(position >= lag_rows, jnp.ones_like(carry_rows), carry_rows)
        for lag_rows in range(conv_x_w.shape[1])
    ]
    x_conv = causal_conv(x_pre, conv_x_w, conv_x_b, keep_masks)
    bc_conv = causal_conv(bc_pre, conv_bc_w, conv_bc_b, keep_masks)
    state_in = bc_conv[:, :STATE].reshape(slot_count, BLOCK, STATE)
    state_out = bc_conv[:, STATE:].reshape(slot_count, BLOCK, STATE)
    inputs = x_conv.reshape(slot_count, BLOCK, head_count, HEADDIM)
    steps_dt = jax.nn.softplus(dt_raw + dt_bias[None, :]) * token_mask[:, None]
    decay_rates = (steps_dt * (-jnp.exp(a_log))[None, :]).reshape(slot_count, BLOCK, head_count)
    steps_three = steps_dt.reshape(slot_count, BLOCK, head_count)
    lower_mask = (jnp.arange(BLOCK)[:, None] >= jnp.arange(BLOCK)[None, :]).astype(x_pre.dtype)
    cumulative = jnp.einsum("ij,sjh->sih", lower_mask, decay_rates, precision=HIGHEST_PREC)
    scores_cb = jnp.einsum("sin,sjn->sij", state_out, state_in, precision=HIGHEST_PREC)
    differ = cumulative[:, :, None, :] - cumulative[:, None, :, :]
    decay_mat = jnp.exp(jnp.where(lower_mask[None, :, :, None] > 0.5, differ, -1e30))
    mixing = scores_cb[:, :, :, None] * decay_mat * steps_three[:, None, :, :]
    y_local = jnp.einsum("sijh,sjhp->sihp", mixing, inputs, precision=HIGHEST_PREC)
    span_total = cumulative[:, -1, :]
    to_end = jnp.exp(span_total[:, None, :] - cumulative) * steps_three
    block_states = jnp.einsum(
        "sjn,sjh,sjhp->shnp", state_in, to_end, inputs, precision=HIGHEST_PREC
    )
    carried = []
    current = jnp.zeros((head_count, STATE, HEADDIM), x_pre.dtype)
    for slot_index in range(slot_count):
        current = current * carry_flags[slot_index]
        carried.append(current)
        current = (
            current * jnp.exp(span_total[slot_index])[:, None, None] + block_states[slot_index]
        )
    entering = jnp.stack(carried)
    y_state = (
        jnp.einsum("sin,shnp->sihp", state_out, entering, precision=HIGHEST_PREC)
        * jnp.exp(cumulative)[:, :, :, None]
    )
    output = y_local + y_state + inputs * d_skip[None, None, :, None]
    return output.reshape(row_count, head_count * HEADDIM)


def dot_nt(left, right):
    return lax.dot_general(
        left, right, (((1,), (1,)), ((), ())), preferred_element_type=jnp.float32
    )


def dot_tn(left, right):
    return lax.dot_general(
        left, right, (((0,), (0,)), ((), ())), preferred_element_type=jnp.float32
    )


def per_device(
    tokens,
    norm_gain,
    w_z,
    w_x,
    w_dt,
    w_bc,
    w_out,
    conv_x_w,
    conv_x_b,
    conv_bc_w,
    conv_bc_b,
    a_log,
    d_skip,
    dt_bias,
    norm_w,
    block_seq,
    block_len,
    cotangent,
):
    bc_full, gain_full, conv_bcw_full, conv_bcb_full = (
        lax.all_gather(w_bc.astype(jnp.float32), ("dp", "tensor"), axis=0, tiled=True),
        lax.all_gather(norm_gain, ("dp", "tensor"), axis=0, tiled=True),
        lax.all_gather(conv_bc_w, ("dp", "tensor"), axis=0, tiled=True),
        lax.all_gather(conv_bc_b, ("dp", "tensor"), axis=0, tiled=True),
    )
    bc_weight = bc_full.astype(jnp.bfloat16)
    mean_sq = jnp.mean(tokens * tokens, axis=1, keepdims=True)
    inv_rms = lax.rsqrt(mean_sq + EPSILON)
    unit_rows = tokens * inv_rms
    normed_own = (unit_rows * gain_full[None, :]).astype(jnp.bfloat16)
    normed = lax.all_gather(normed_own, "tensor", axis=0, tiled=True)
    z_full, x_full, dt_full, out_full = (
        lax.all_gather(w_z, "dp", axis=0, tiled=True),
        lax.all_gather(w_x, "dp", axis=0, tiled=True),
        lax.all_gather(w_dt, "dp", axis=0, tiled=True),
        lax.all_gather(w_out, "dp", axis=0, tiled=True),
    )
    row_count = normed.shape[0]
    slot_count = block_seq.shape[0]
    slot_index = jnp.arange(slot_count)
    previous = jnp.concatenate([block_seq[:1] - 1, block_seq[:-1]])
    carry_flags = ((slot_index > 0) & (block_seq == previous)).astype(jnp.float32)
    token_mask = (jnp.arange(row_count) % BLOCK < jnp.repeat(block_len, BLOCK)).astype(jnp.float32)
    gate_pre = jnp.dot(normed, z_full, preferred_element_type=jnp.float32)
    x_pre = jnp.dot(normed, x_full, preferred_element_type=jnp.float32)
    bc_pre = jnp.dot(normed, bc_weight, preferred_element_type=jnp.float32)
    dt_raw = jnp.dot(normed, dt_full, preferred_element_type=jnp.float32)

    def local_scan(xp_in, bc_in, dt_in, cxw, cxb, cbw, cbb, alog_in, skip_in, bias_in):
        return scan_heads(
            xp_in,
            bc_in,
            dt_in,
            cxw,
            cxb,
            cbw,
            cbb,
            alog_in,
            skip_in,
            bias_in,
            carry_flags,
            token_mask,
        )

    y_local, scan_back = jax.vjp(
        local_scan,
        x_pre,
        bc_pre,
        dt_raw,
        conv_x_w,
        conv_x_b,
        conv_bcw_full,
        conv_bcb_full,
        a_log,
        d_skip,
        dt_bias,
    )
    gated_rows = y_local * jax.nn.silu(gate_pre)
    sq_sum = lax.psum(jnp.sum(gated_rows * gated_rows, axis=1), "tensor")
    inv_g = lax.rsqrt(sq_sum[:, None] / INNER + EPSILON)
    unit_g = gated_rows * inv_g
    hidden = (unit_g * norm_w[None, :] * token_mask[:, None]).astype(jnp.bfloat16)
    branch = lax.psum_scatter(
        dot_nt(hidden, out_full).astype(jnp.bfloat16), "tensor", scatter_dimension=0, tiled=True
    ).astype(jnp.float32)
    output = tokens + branch
    cot_rows = lax.all_gather(cotangent.astype(jnp.bfloat16), "tensor", axis=0, tiled=True)
    z_back, x_back, dt_back, out_back = (z_full, x_full, dt_full, out_full)
    d_hidden = jnp.dot(cot_rows, out_back, preferred_element_type=jnp.float32)
    g_w_out = lax.psum_scatter(dot_tn(cot_rows, hidden), "dp", scatter_dimension=0, tiled=True)
    d_unit = d_hidden * norm_w[None, :] * token_mask[:, None]
    g_norm_w = jnp.sum(d_hidden * unit_g * token_mask[:, None], axis=0)
    inner_sum = lax.psum(jnp.sum(d_unit * unit_g, axis=1), "tensor")
    d_gated = inv_g * (d_unit - unit_g * inner_sum[:, None] / INNER)
    sigmoid_gate = jax.nn.sigmoid(gate_pre)
    d_y = d_gated * gate_pre * sigmoid_gate
    d_gate = d_gated * y_local * sigmoid_gate * (1.0 + gate_pre * (1.0 - sigmoid_gate))
    d_xp, d_bc, d_dt, g_cxw, g_cxb, g_cbw, g_cbb, g_alog, g_skip, g_bias = scan_back(d_y)
    gate_g = d_gate.astype(jnp.bfloat16)
    x_g = d_xp.astype(jnp.bfloat16)
    dt_g = d_dt.astype(jnp.bfloat16)
    bc_g = d_bc.astype(jnp.bfloat16)
    joined = jnp.concatenate([gate_g, x_g, dt_g], axis=1)
    in_grads = lax.psum_scatter(dot_tn(normed, joined), "dp", scatter_dimension=0, tiled=True)
    width_local = w_z.shape[1]
    g_w_z = in_grads[:, :width_local]
    g_w_x = in_grads[:, width_local : 2 * width_local]
    g_w_dt = in_grads[:, 2 * width_local :]
    g_w_bc_part = dot_tn(normed, bc_g)
    summed = dot_nt(gate_g, z_back) + dot_nt(x_g, x_back)
    d_normed = lax.psum_scatter(
        summed + dot_nt(dt_g, dt_back) + dot_nt(bc_g, bc_weight),
        "tensor",
        scatter_dimension=0,
        tiled=True,
    )
    g_gain_part = jnp.sum(d_normed * unit_rows, axis=0)
    d_unit_r = d_normed * gain_full[None, :]
    d_tokens = cotangent + inv_rms * (
        d_unit_r - unit_rows * jnp.mean(d_unit_r * unit_rows, axis=1, keepdims=True)
    )
    g_w_bc, g_gain, g_conv_bcw, g_conv_bcb = (
        lax.psum_scatter(g_w_bc_part, ("dp", "tensor"), scatter_dimension=0, tiled=True),
        lax.psum_scatter(g_gain_part, ("dp", "tensor"), scatter_dimension=0, tiled=True),
        lax.psum_scatter(g_cbw, ("dp", "tensor"), scatter_dimension=0, tiled=True),
        lax.psum_scatter(g_cbb, ("dp", "tensor"), scatter_dimension=0, tiled=True),
    )
    g_cxw, g_cxb, g_alog, g_skip, g_bias, g_norm_w = lax.psum(
        (g_cxw, g_cxb, g_alog, g_skip, g_bias, g_norm_w), "dp"
    )
    return (
        output,
        d_tokens,
        g_gain,
        g_w_z,
        g_w_x,
        g_w_dt,
        g_w_bc,
        g_w_out,
        g_cxw,
        g_cxb,
        g_conv_bcw,
        g_conv_bcb,
        g_alog,
        g_skip,
        g_bias,
        g_norm_w,
    )


def solution(mesh):
    return jax.shard_map(
        per_device,
        mesh=mesh,
        in_specs=(
            P(("dp", "tensor"), None),
            P(("dp", "tensor")),
            P("dp", "tensor"),
            P("dp", "tensor"),
            P("dp", "tensor"),
            P(("dp", "tensor"), None),
            P("dp", "tensor"),
            P("tensor", None),
            P("tensor"),
            P(("dp", "tensor"), None),
            P(("dp", "tensor")),
            P("tensor"),
            P("tensor"),
            P("tensor"),
            P("tensor"),
            P("dp"),
            P("dp"),
            P(("dp", "tensor"), None),
        ),
        out_specs=(
            P(("dp", "tensor"), None),
            P(("dp", "tensor"), None),
            P(("dp", "tensor")),
            P("dp", "tensor"),
            P("dp", "tensor"),
            P("dp", "tensor"),
            P(("dp", "tensor"), None),
            P("dp", "tensor"),
            P("tensor", None),
            P("tensor"),
            P(("dp", "tensor"), None),
            P(("dp", "tensor")),
            P("tensor"),
            P("tensor"),
            P("tensor"),
            P("tensor"),
        ),
        check_vma=False,
    )
```

profile of v0, /device:TPU:0, one launch (start us, length us, event | category | flops | bytes accessed | tf_op | source)
XLA Modules:
  0.0 879.1 jit_solution(2588290233400417949)
XLA Ops:
  7.3 1.9 multiply_reduce_fusion.13
  10.9 42.0 %all-reduce.35 = (f32[1024]{0:T(1024)S(1)}, f32[256]{0:T(256)}) all-reduce(f32[1024]{0:T(1024)S(1)} %dynamic-update-slice, f32[256]{0:T(256)S(1)} %dynamic-update-slice.1), channel_id=1, replica_groups=mesh['dp'=16,'tensor'=2] {'dp','tensor'}, use_global_device_ids=true, to_apply=%add.29 | all-reduce | flops 1280 | bytes 10240
  53.0 2.9 multiply_convert_fusion.2
  60.5 21.4 %all-gather.1 = bf16[16,64,16]{1,2,0:T(8,128)(2,1)S(1)} all-gather(bf16[1,64,16]{1,2,0:T(8,128)(2,1)S(1)} %bitcast.308), channel_id=1, replica_groups=mesh['dp'=16,'tensor'=2] {'dp'}, dimensions={0}, use_global_device_ids=true | all-gather | bytes 34816 | tf_op jit(solution)/shard_map/all_gather | solution.py:140
  82.1 64.5 %all-gather = f32[32,8,4]{1,2,0:T(4,128)S(1)} all-gather(f32[1,8,4]{1,2,0:T(4,128)S(1)} %bitcast.309), channel_id=1, replica_groups=mesh['dp'=16,'tensor'=2] {'dp','tensor'}, dimensions={0}, use_global_device_ids=true | all-gather | bytes 4224 | tf_op jit(solution)/shard_map/all_gather | solution.py:128
  146.7 70.3 %all_gather.34 = bf16[1024,256]{1,0:T(8,128)(2,1)S(1)} all-gather(bf16[32,256]{1,0:T(8,128)(2,1)S(1)} %copy-done.52), channel_id=1, replica_groups=mesh['dp'=16,'tensor'=2] {'dp','tensor'}, dimensions={0}, use_global_device_ids=true | all-gather | bytes 540672 | tf_op jit(solution)/shard_map/all_gather | solution.py:126
  218.3 2.9 broadcast_multiply_fusion
  223.2 2.3 fusion.163
  225.5 1.4 fusion.87
  227.0 2.0 fusion.157
  229.0 4.7 fusion.156
  233.7 6.9 fusion.36
  240.6 5.6 reshape.333
  246.3 6.7 fusion.68
  253.1 2.3 fusion.88
  256.5 3.5 fusion.158
  260.0 1.9 copy-done.12
  262.0 19.7 %fusion.35 = f32[4,256,16,64]{1,3,2,0:T(8,128)S(1)} fusion(f32[4,256,16,64]{1,3,2,0:T(8,128)S(1)} %bitcast.260, f32[4,256,16,64]{1,0,3,2:T(4,128)S(1)} %copy-done.6, f32[4,256,16]{1,2,0:T(8,128)S(1)} %bitcast.279, f32[4,256,16]{1,2,0:T(8,128)S(1)} %convolution_bitcast_fusion.2, f32[4,256,256]{2,1,0:T(8,128)S(1)} %copy-done.30, ...), kind=kOutput, calls=%fused_computation.44 | convolution fusion | flops 3242196992 | bytes 13893696 | tf_op jit(solution)/shard_map/jvp(sijh,sjhp->sihp)/dot_general | solution.py:70
  281.6 2.8 copy.106
  284.4 3.0 copy.140
  287.5 10.0 %multiply_reduce_fusion.10 = (f32[1024]{0:T(1024)S(1)}, f32[1024,1024]{0,1:T(8,128)}, f32[1024,1024]{0,1:T(8,128)}) fusion(f32[1024,1024]{0,1:T(8,128)} %bitcast.255, bf16[1024,1024]{1,0:T(8,128)(2,1)} %all-gather.8.cloned.1.call-done, bf16[1024,1024]{1,0:T(8,128)(2,1)} %all-gather.12.cloned.1.call-done), kind=kOutput, calls=%fused_computation.61 | convolution fusion | flops 2154822656 | bytes 16781312 | tf_op jit(solution)/shard_map/dot_general | solution.py:149
  297.5 4.9 psum.56
  302.5 9.4 %multiply_reduce_fusion.2 = (f32[1024]{0:T(1024)}, f32[1024]{0:T(1024)S(1)}, f32[1024,1024]{0,1:T(8,128)}) fusion(f32[1024,1024]{0,1:T(8,128)} %get-tuple-element.126, f32[1024]{0:T(1024)S(1)} %fusion.133, f32[1024]{0:T(1024)S(1)} %add_rsqrt_fusion, f32[1024]{0:T(1024)S(1)} %copy-done.69, bf16[1024,1024]{1,0:T(8,128)(2,1)} %all-gather.16.cloned.1.call-done, ...), kind=kOutput, calls=%fused_computation.46 | convolution fusion | flops 2155870208 | bytes 12603392 | tf_op jit(solution)/shard_map/dot_general | solution.py:194
  311.9 4.9 psum.57
  316.8 11.7 %multiply_reduce_fusion.3 = (f32[1024]{0:T(1024)}, f32[1024,1024]{0,1:T(8,128)}, bf16[1024,1024]{0,1:T(8,128)(2,1)}) fusion(f32[1024,1024]{0,1:T(8,128)} %get-tuple-element.133, f32[1024,1024]{0,1:T(8,128)} %get-tuple-element.165, f32[1024]{0:T(1024)S(1)} %psum.57, f32[1024,1024]{0,1:T(8,128)} %get-tuple-element.126, f32[1024]{0:T(1024)S(1)} %fusion.133, ...), kind=kLoop, calls=%fused_computation.47 | loop fusion | flops 26213376 | bytes 27283456 | tf_op jit(solution)/shard_map/transpose(jvp())/reduce_sum | solution.py:89
  328.4 5.7 reshape.339
  334.1 4.9 multiply_reduce_fusion.8
  339.2 7.0 fusion.79
  346.2 27.4 %fusion.8 = (f32[4,256,16]{1,2,0:T(8,128)}, f32[4,256,16]{1,2,0:T(8,128)}, f32[4,256,16]{1,2,0:T(8,128)}, f32[4,256,256]{2,1,0:T(8,128)S(1)}) fusion(f32[4,256,16]{1,2,0:T(8,128)S(1)} %bitcast.280, f32[4,256,16]{1,2,0:T(8,128)S(1)} %convolution_bitcast_fusion.2, f32[4,256,256]{2,1,0:T(8,128)S(1)} %copy-done.31, pred[256,256]{1,0:T(8,128)(4,1)S(1)} %copy-done.34, ...), kind=kOutput, calls=%fused_computation.11 | convolution fusion | flops 3275440128 | bytes 10878976 | tf_op jit(solution)/shard_map/transpose(jvp(sijh,sjhp->sihp))/dot_general | solution.py:70
  373.6 4.2 fusion.71
  377.9 3.1 fusion.93
  381.0 1.5 add_multiply_fusion
  382.5 6.8 fusion.74
  389.3 4.0 fusion.62
  393.3 3.7 multiply_reduce_fusion.1
  397.1 15.7 %bitcast_add_fusion = f32[4,256,16,64]{1,3,2,0:T(8,128)S(1)} fusion(f32[4,256,16,64]{1,3,2,0:T(8,128)S(1)} %fusion.62, f32[4,256,16,64]{1,0,3,2:T(4,128)S(1)} %copy-done.9, f32[4,256,16]{1,2,0:T(8,128)S(1)} %bitcast.281, f32[4,256,16]{1,2,0:T(8,128)S(1)} %convolution_bitcast_fusion.2, f32[4,256,256]{2,1,0:T(8,128)S(1)} %copy-done.31, ...), kind=kOutput, calls=%fused_computation.39 | convolution fusion | flops 3242196992 | bytes 13893696 | tf_op jit(solution)/shard_map/transpose(jvp(sijh,sjhp->sihp))/dot_general | solution.py:70
  413.9 1.9 convolution_add_fusion
  415.8 2.3 fusion.144
  419.5 2.8 copy.110
  424.5 1.3 copy-done.8
  425.8 6.4 fusion.143
  432.2 3.3 fusion.29
  435.5 3.4 fusion.30
  438.9 1.2 fusion.86
  440.2 3.4 fusion.31
  446.5 1.7 add_convert_fusion.1
  449.2 1.3 copy-done.11
  450.5 4.6 add_convert_fusion
  455.2 2.4 fusion.159
  457.6 2.4 fusion.160
  460.0 2.9 add_add_fusion
  463.6 7.5 convolution_convert_fusion
  471.4 10.8 %fusion.21 = f32[1024,2064]{1,0:T(8,128)} fusion(bf16[1024,1024]{1,0:T(8,128)(2,1)} %all-gather.8.cloned.1.call-done, bf16[1024,16]{0,1:T(8,128)(2,1)S(1)} %get-tuple-element.117, bf16[1024,1024]{0,1:T(8,128)(2,1)} %copy-done.18, bf16[1024,1024]{0,1:T(8,128)(2,1)S(1)} %copy-done.17), kind=kOutput, calls=%fused_computation.25 | convolution fusion | flops 4341202944 | bytes 14778368 | tf_op jit(solution)/shard_map/dot_general | solution.py:100
  483.9 1.7 fusion.161
  485.7 7.2 convolution_bitcast_fusion
  493.0 5.4 copy.130
  499.4 57.7 %all-reduce.36 = (f32[1024,4]{0,1:T(4,128)}, f32[1024]{0:T(1024)}, f32[16]{0:T(128)}, f32[16]{0:T(128)}, f32[16]{0:T(128)}, /*index=5*/f32[1024]{0:T(1024)}) all-reduce(f32[1024,4]{0,1:T(4,128)S(1)} %pad_add_fusion.3, f32[1024]{0:T(1024)S(1)} %copy-done.45, ...), channel_id=1, replica_groups=mesh['dp'=16,'tensor'=2] {'dp'}, use_global_device_ids=true, to_apply=%region_26.27 | all-reduce | flops 6192 | bytes 49536 | tf_op jit(solution)/shard_map/psum | solution.py:233
  557.1 2.3 multiply_reduce_fusion.11
  559.5 38.5 %all-reduce.34 = (f32[1024]{0:T(1024)S(1)}, f32[256,4]{0,1:T(4,128)S(1)}, f32[256]{0:T(256)S(1)}) all-reduce(f32[1024]{0:T(1024)S(1)} %get-tuple-element.86, f32[256,4]{0,1:T(4,128)S(1)} %pad_add_fusion.4, f32[256]{0:T(256)S(1)} %copy-done.71), channel_id=4, replica_groups=mesh['dp'=16,'tensor'=2] {'dp','tensor'}, use_global_device_ids=true, to_apply=%region_18.19.clone | all-reduce | flops 2304 | bytes 18432
  599.8 5.2 multiply_add_fusion.1
  605.0 54.9 %reduce-scatter.13.cloned.1.call-done = f32[64,2064]{1,0:T(8,128)} async-done(((f32[1024,2064]{1,0:T(8,128)}), f32[64,2064]{1,0:T(8,128)}) %reduce-scatter.13.cloned.1.call-update) | async-done | bytes 528400 | tf_op jit(solution)/shard_map/reduce_scatter | solution.py:209
  661.3 1.9 fusion.151
  663.2 135.9 %reduce-scatter.15.cloned.1.call-done = f32[32,256]{1,0:T(8,128)} async-done(((f32[1024,256]{1,0:T(8,128)}), f32[32,256]{1,0:T(8,128)}) %reduce-scatter.15.cloned.1.call-update) | async-done | bytes 32784 | tf_op jit(solution)/shard_map/reduce_scatter | solution.py:228
  799.1 73.0 %reduce-scatter.17.cloned.1.call-done = f32[64,1024]{1,0:T(8,128)} async-done(((f32[1024,1024]{1,0:T(8,128)}), f32[64,1024]{1,0:T(8,128)}) %reduce-scatter.17.cloned.1.call-update) | async-done | bytes 262160
  (277 shorter events, 25.9 us)
Async XLA Ops:
  7.2 53.0 %copy-start = (s32[4]{0:T(128)S(1)}, s32[4]{0:T(128)}, u32[]{:S(2)}) copy-start(s32[4]{0:T(128)} %param.34) | copy-start | bytes 52
  7.2 50.2 %copy-start.15 = (f32[512,1024]{1,0:T(8,128)S(1)}, f32[512,1024]{1,0:T(8,128)}, u32[]{:S(2)}) copy-start(f32[512,1024]{1,0:T(8,128)} %param.35) | copy-start | bytes 6291460
  7.2 211.1 %all-gather.8.cloned.1.call-start = ((), (), s32[]{:S(2)}) async-start(), calls=%async_computation.5 | async-start | bytes 3145728 | tf_op jit(solution)/shard_map/all_gather | solution.py:136
  9.2 49.4 %copy-start.40 = (f32[512]{0:T(512)}, f32[512]{0:T(512)S(1)}, u32[]{:S(2)}) copy-start(f32[512]{0:T(512)S(1)} %add_rsqrt_fusion.1) | copy-start | bytes 6148
  53.0 5.6 copy-start.38
  53.0 6.3 copy-start.83
  53.0 7.1 copy-start.95
  53.0 7.5 copy-start.53
  53.0 7.5 copy-start.76
  53.0 29.1 %copy-start.81 = (f32[8,4]{0,1:T(4,128)S(1)}, f32[8,4]{0,1:T(4,128)}, u32[]{:S(2)}) copy-start(f32[8,4]{0,1:T(4,128)} %param.27) | copy-start | bytes 388
  53.0 93.7 %copy-start.52 = (bf16[32,256]{1,0:T(8,128)(2,1)S(1)}, bf16[32,256]{1,0:T(8,128)(2,1)}, u32[]{:S(2)}) copy-start(bf16[32,256]{1,0:T(8,128)(2,1)} %param.23) | copy-start | bytes 49156
  55.9 162.4 %copy-start.88 = (f32[16]{0:T(128)S(1)}, f32[16]{0:T(128)}, u32[]{:S(2)}) copy-start(f32[16]{0:T(128)} %param.31) | copy-start | bytes 196
  55.9 173.1 %all-gather.10.cloned.1.call-start = ((), (), s32[]{:S(2)}) async-start(), calls=%async_computation.6 | async-start | bytes 2228224 | tf_op jit(solution)/shard_map/all_gather | solution.py:139
  56.6 230.8 %all-gather.12.cloned.1.call-start = ((), (), s32[]{:S(2)}) async-start(), calls=%async_computation.7 | async-start | bytes 2228224 | tf_op jit(solution)/shard_map/all_gather | solution.py:138
  57.4 245.1 %all-gather.16.cloned.1.call-start = ((), (), s32[]{:S(2)}) async-start(), calls=%async_computation.10 | async-start | bytes 3145728 | tf_op jit(solution)/shard_map/all_gather | solution.py:192
  58.6 243.9 %all-gather.14.cloned.1.call-start = ((), (), s32[]{:S(2)}) async-start(), calls=%async_computation.8 | async-start | bytes 2228224 | tf_op jit(solution)/shard_map/all_gather | solution.py:141
  59.2 497.9 %reduce-scatter.11.cloned.1.call-start = ((), (), s32[]{:S(2)}) async-start(), calls=%async_computation.11 | async-start | bytes 6291456 | tf_op jit(solution)/shard_map/reduce_scatter | solution.py:216
  60.1 199.9 %copy-start.33 = (pred[256,256]{1,0:T(8,128)(4,1)}, pred[256,256]{1,0:T(8,128)(4,1)S(1)}, u32[]{:S(2)}) copy-start(pred[256,256]{1,0:T(8,128)(4,1)S(1)} %convert_compare_fusion) | copy-start | bytes 196612
  60.1 161.1 %copy-start.84 = (f32[16]{0:T(128)}, f32[16]{0:T(128)S(1)}, u32[]{:S(2)}) copy-start(f32[16]{0:T(128)S(1)} %exponential_negate_fusion) | copy-start | bytes 196
  146.7 78.8 %copy-start.57 = (f32[256,1]{0,1:T(1,128)}, f32[256,1]{0,1:T(1,128)S(1)}, u32[]{:S(2)}) copy-start(f32[256,1]{0,1:T(1,128)S(1)} %get-tuple-element.157) | copy-start | bytes 3076
  146.7 78.8 %copy-start.58 = (f32[256,1]{0,1:T(1,128)}, f32[256,1]{0,1:T(1,128)S(1)}, u32[]{:S(2)}) copy-start(f32[256,1]{0,1:T(1,128)S(1)} %get-tuple-element.158) | copy-start | bytes 3076
  146.7 78.8 %copy-start.60 = (f32[256,1]{0,1:T(1,128)}, f32[256,1]{0,1:T(1,128)S(1)}, u32[]{:S(2)}) copy-start(f32[256,1]{0,1:T(1,128)S(1)} %get-tuple-element.159) | copy-start | bytes 3076
  146.7 78.8 %copy-start.62 = (f32[256,1]{0,1:T(1,128)}, f32[256,1]{0,1:T(1,128)S(1)}, u32[]{:S(2)}) copy-start(f32[256,1]{0,1:T(1,128)S(1)} %get-tuple-element.156) | copy-start | bytes 3076
  217.1 8.4 copy-start.21
  218.3 7.3 copy-start.86
  221.6 5.3 copy-start.42
  229.0 4.7 copy-start.78
  233.7 6.9 copy-start.2
  246.3 6.7 copy-start.54
  246.3 6.7 copy-start.64
  246.3 6.8 copy-start.67
  246.3 9.1 %copy-start.89 = (f32[4]{0:T(128)S(1)}, f32[4]{0:T(128)}, u32[]{:S(2)}) copy-start(f32[4]{0:T(128)} %pad.101.clone) | copy-start | bytes 52
  253.0 7.0 copy-start.13
  256.5 5.5 copy-start.6
  256.5 5.5 copy-start.30
  256.5 5.5 copy-start.35
  256.5 5.5 copy-start.93
  287.5 15.0 %copy-start.69 = (f32[1024]{0:T(1024)S(1)}, f32[1024]{0:T(1024)}, u32[]{:S(2)}) copy-start(f32[1024]{0:T(1024)} %param.32) | copy-start | bytes 12292
  302.4 14.3 %copy-start.46 = (f32[1024]{0:T(1024)}, f32[1024]{0:T(1024)S(1)}, u32[]{:S(2)}) copy-start(f32[1024]{0:T(1024)S(1)} %add_rsqrt_fusion) | copy-start | bytes 12292
  334.1 4.9 copy-start.9
  334.1 4.9 copy-start.25
  334.1 4.9 copy-start.27
  334.1 5.1 copy-start.29
  334.1 5.1 copy-start.90
  339.2 7.0 copy-start.7
  339.2 7.0 copy-start.31
  339.2 7.0 copy-start.34
  339.2 7.0 copy-start.36
  432.2 7.9 copy-start.4
  440.2 6.3 copy-start.16
  450.5 4.7 copy-start.92
  462.9 136.9 %reduce-scatter.9.cloned.1.call-start = ((), (), s32[]{:S(2)}) async-start(), calls=%async_computation.9 | async-start | bytes 3145728 | tf_op jit(solution)/shard_map/reduce_scatter | solution.py:188
  471.2 188.8 %reduce-scatter.13.cloned.1.call-start = ((), (), s32[]{:S(2)}) async-start(), calls=%async_computation.12 | async-start | bytes 9469952 | tf_op jit(solution)/shard_map/reduce_scatter | solution.py:209
  482.2 316.9 %reduce-scatter.15.cloned.1.call-start = ((), (), s32[]{:S(2)}) async-start(), calls=%async_computation.13 | async-start | bytes 1081344 | tf_op jit(solution)/shard_map/reduce_scatter | solution.py:228
  485.7 386.4 %reduce-scatter.17.cloned.1.call-start = ((), (), s32[]{:S(2)}) async-start(), calls=%async_computation.14 | async-start | bytes 4456448
  498.5 58.6 %copy-start.72 = (f32[256]{0:T(256)S(1)}, f32[256]{0:T(256)}, u32[]{:S(2)}) copy-start(f32[256]{0:T(256)} %get-tuple-element.97) | copy-start | bytes 3076
  498.5 58.6 %copy-start.73 = (f32[256]{0:T(256)S(1)}, f32[256]{0:T(256)}, u32[]{:S(2)}) copy-start(f32[256]{0:T(256)} %get-tuple-element.98) | copy-start | bytes 3076
  498.5 58.6 %copy-start.74 = (f32[256]{0:T(256)S(1)}, f32[256]{0:T(256)}, u32[]{:S(2)}) copy-start(f32[256]{0:T(256)} %get-tuple-element.99) | copy-start | bytes 3076
  498.5 58.6 %copy-start.75 = (f32[256]{0:T(256)S(1)}, f32[256]{0:T(256)}, u32[]{:S(2)}) copy-start(f32[256]{0:T(256)} %get-tuple-element.100) | copy-start | bytes 3076
  498.5 58.6 %copy-start.10 = (f32[512,1024]{1,0:T(8,128)S(1)}, f32[512,1024]{1,0:T(8,128)}, u32[]{:S(2)}) copy-start(f32[512,1024]{1,0:T(8,128)} %param.18) | copy-start | bytes 6291460
  498.5 58.6 %copy-start.39 = (f32[1024]{0:T(1024)S(1)}, f32[1024]{0:T(1024)}, u32[]{:S(2)}) copy-start(f32[1024]{0:T(1024)} %copy-done.38) | copy-start | bytes 12292
  498.5 58.6 %copy-start.41 = (f32[512]{0:T(512)S(1)}, f32[512]{0:T(512)}, u32[]{:S(2)}) copy-start(f32[512]{0:T(512)} %copy-done.40) | copy-start | bytes 6148
  498.5 61.0 %copy-start.71 = (f32[256]{0:T(256)S(1)}, f32[256]{0:T(256)}, u32[]{:S(2)}) copy-start(f32[256]{0:T(256)} %get-tuple-element.96) | copy-start | bytes 3076
  599.8 272.3 %copy-start.1 = (s32[4]{0:T(128)S(1)}, s32[4]{0:T(128)}, u32[]{:S(2)}) copy-start(s32[4]{0:T(128)} %param.34) | copy-start | bytes 52
  (43 other events, 106.9 us)
Sparse Core Ops, SparseCore 0:
  56.0 33.3 all-gather.7
  91.5 41.5 all-gather.9
  135.3 40.3 all-gather.11
  177.1 35.7 all-gather.15
  214.9 41.4 all-gather.13
  463.0 50.2 reduce-scatter.10
  516.1 31.8 reduce-scatter.8
  552.2 107.7 reduce-scatter.12
  662.7 136.3 reduce-scatter.14
  803.4 68.6 reduce-scatter.16
where the time goes:
time: 883 us; the launch traced here: 879 us
  blocking collectives  304 us (34%)
  waiting for transfers between devices  266 us (30%)
  matrix products  166 us (19%)
  other arithmetic  79 us (9%)
  local copies, waits for them, and re-layouts  46.8 us (5%)
  between operations  16.3 us (2%)
    reduce_scatter x1, waiting for transfers between devices, per_device(): lax.psum_scatter(g_w_bc_part, ('dp', 'tensor'), scatter_dimension=0, tile...  136 us
    unnamed x2, blocking collectives  80.5 us
    unnamed x11, waiting for transfers between devices  75 us
    all_gather x1, blocking collectives, per_device(): lax.all_gather(w_bc.astype(jnp.float32), ('dp', 'tensor'), axis=0, tiled=...  70.3 us
    all_gather x1, blocking collectives, per_device(): lax.all_gather(conv_bc_w, ('dp', 'tensor'), axis=0, tiled=True)  64.5 us
    dot_general x3, matrix products, scan_heads(): jnp.einsum('sijh,sjhp->sihp', mixing, inputs, precision=HIGHEST_PREC)  62.8 us
    psum x1, blocking collectives, per_device(): lax.psum((g_cxw, g_cxb, g_alog, g_skip, g_bias, g_norm_w), 'dp')  57.7 us
    reduce_scatter x1, waiting for transfers between devices, per_device(): lax.psum_scatter(dot_tn(normed, joined), 'dp', scatter_dimension=0, tiled...  54.9 us
  transfers between devices with their start and end apart: 10, of which 3 were waited for; matrix products, arithmetic and copies ran while one was open for 14% of the time, Pallas kernels for 0%

commit v1 on v0

--- a/solution.py
+++ b/solution.py
@@ -11,6 +11,7 @@
 
 EPSILON = 1e-05
 HIGHEST_PREC = lax.Precision.HIGHEST
+HIGH_PREC = lax.Precision.HIGH
 
 
 def shift_rows(values, lag_rows):
@@ -63,15 +64,15 @@
     steps_three = steps_dt.reshape(slot_count, BLOCK, head_count)
     lower_mask = (jnp.arange(BLOCK)[:, None] >= jnp.arange(BLOCK)[None, :]).astype(x_pre.dtype)
     cumulative = jnp.einsum("ij,sjh->sih", lower_mask, decay_rates, precision=HIGHEST_PREC)
-    scores_cb = jnp.einsum("sin,sjn->sij", state_out, state_in, precision=HIGHEST_PREC)
+    scores_cb = jnp.einsum("sin,sjn->sij", state_out, state_in, precision=HIGH_PREC)
     differ = cumulative[:, :, None, :] - cumulative[:, None, :, :]
     decay_mat = jnp.exp(jnp.where(lower_mask[None, :, :, None] > 0.5, differ, -1e30))
     mixing = scores_cb[:, :, :, None] * decay_mat * steps_three[:, None, :, :]
-    y_local = jnp.einsum("sijh,sjhp->sihp", mixing, inputs, precision=HIGHEST_PREC)
+    y_local = jnp.einsum("sijh,sjhp->sihp", mixing, inputs, precision=HIGH_PREC)
     span_total = cumulative[:, -1, :]
     to_end = jnp.exp(span_total[:, None, :] - cumulative) * steps_three
     block_states = jnp.einsum(
-        "sjn,sjh,sjhp->shnp", state_in, to_end, inputs, precision=HIGHEST_PREC
+        "sjn,sjh,sjhp->shnp", state_in, to_end, inputs, precision=HIGH_PREC
     )
     carried = []
     current = jnp.zeros((head_count, STATE, HEADDIM), x_pre.dtype)
@@ -83,7 +84,7 @@
         )
     entering = jnp.stack(carried)
     y_state = (
-        jnp.einsum("sin,shnp->sihp", state_out, entering, precision=HIGHEST_PREC)
+        jnp.einsum("sin,shnp->sihp", state_out, entering, precision=HIGH_PREC)
         * jnp.exp(cumulative)[:, :, :, None]
     )
     output = y_local + y_state + inputs * d_skip[None, None, :, None]
@@ -100,6 +101,23 @@
     return lax.dot_general(
         left, right, (((0,), (0,)), ((), ())), preferred_element_type=jnp.float32
     )
+
+
+def tensor_scatter_sum(parts):
+    size = parts.shape[0]
+    own = lax.axis_index("tensor")
+    total = lax.dynamic_index_in_dim(parts, own, 0, keepdims=False)
+    for step in range(1, size):
+        outgoing = lax.dynamic_index_in_dim(parts, (own + step) % size, 0, keepdims=False)
+        ring = [(source, (source + step) % size) for source in range(size)]
+        total = total + lax.ppermute(outgoing, "tensor", ring)
+    return total
+
+
+def scatter_dp(values):
+    return lax.psum_scatter(
+        values.astype(jnp.bfloat16), "dp", scatter_dimension=0, tiled=True
+    ).astype(jnp.float32)
 
 
 def per_device(
@@ -122,24 +140,45 @@
     block_len,
     cotangent,
 ):
-    bc_full, gain_full, conv_bcw_full, conv_bcb_full = (
-        lax.all_gather(w_bc.astype(jnp.float32), ("dp", "tensor"), axis=0, tiled=True),
-        lax.all_gather(norm_gain, ("dp", "tensor"), axis=0, tiled=True),
-        lax.all_gather(conv_bc_w, ("dp", "tensor"), axis=0, tiled=True),
-        lax.all_gather(conv_bc_b, ("dp", "tensor"), axis=0, tiled=True),
-    )
-    bc_weight = bc_full.astype(jnp.bfloat16)
+    dp_size = lax.axis_size("dp")
+    tensor_size = lax.axis_size("tensor")
+    bc_rows, bc_width = w_bc.shape
+    width_local = w_z.shape[1]
+    weight_rows = w_z.shape[0]
+    bc_flat = w_bc.reshape(weight_rows, bc_width * bc_rows // weight_rows)
+    bc_cols = bc_flat.shape[1]
+    packed = lax.all_gather(
+        jnp.concatenate([w_z, w_x, bc_flat, w_dt], axis=1), "dp", axis=0, tiled=True
+    )
+    z_full = packed[:, :width_local]
+    x_full = packed[:, width_local : 2 * width_local]
+    bc_own = packed[:, 2 * width_local : 2 * width_local + bc_cols]
+    dt_full = packed[:, 2 * width_local + bc_cols :]
+
+    gain_len, conv_len, taps = norm_gain.shape[0], conv_bc_w.shape[0], conv_bc_w.shape[1]
+    small = jnp.concatenate([norm_gain, conv_bc_w.reshape(-1), conv_bc_b])
+    small_full = lax.all_gather(small, ("dp", "tensor"), axis=0, tiled=False)
+    gain_full = small_full[:, :gain_len].reshape(-1)
+    conv_bcw_full = small_full[:, gain_len : gain_len + conv_len * taps].reshape(-1, taps)
+    conv_bcb_full = small_full[:, gain_len + conv_len * taps :].reshape(-1)
+
     mean_sq = jnp.mean(tokens * tokens, axis=1, keepdims=True)
     inv_rms = lax.rsqrt(mean_sq + EPSILON)
     unit_rows = tokens * inv_rms
     normed_own = (unit_rows * gain_full[None, :]).astype(jnp.bfloat16)
-    normed = lax.all_gather(normed_own, "tensor", axis=0, tiled=True)
-    z_full, x_full, dt_full, out_full = (
-        lax.all_gather(w_z, "dp", axis=0, tiled=True),
-        lax.all_gather(w_x, "dp", axis=0, tiled=True),
-        lax.all_gather(w_dt, "dp", axis=0, tiled=True),
-        lax.all_gather(w_out, "dp", axis=0, tiled=True),
-    )
+    own_rows = normed_own.shape[0]
+    bc_extra = bc_own.reshape(-1, normed_own.shape[1])
+    joined_rows = lax.all_gather(
+        jnp.concatenate([normed_own, bc_extra], axis=0), "tensor", axis=0, tiled=False
+    )
+    normed = joined_rows[:, :own_rows].reshape(-1, normed_own.shape[1])
+    bc_pair = joined_rows[:, own_rows:].reshape(tensor_size, dp_size, bc_rows, bc_width)
+    bc_weight = bc_pair.transpose(1, 0, 2, 3).reshape(-1, bc_width)
+    cot_in, w_out_in, normed = lax.optimization_barrier(
+        (cotangent.astype(jnp.bfloat16), w_out, normed)
+    )
+    cot_rows = lax.all_gather(cot_in, "tensor", axis=0, tiled=True)
+    out_full = lax.all_gather(w_out_in, "dp", axis=0, tiled=True)
     row_count = normed.shape[0]
     slot_count = block_seq.shape[0]
     slot_index = jnp.arange(slot_count)
@@ -185,14 +224,9 @@
     inv_g = lax.rsqrt(sq_sum[:, None] / INNER + EPSILON)
     unit_g = gated_rows * inv_g
     hidden = (unit_g * norm_w[None, :] * token_mask[:, None]).astype(jnp.bfloat16)
-    branch = lax.psum_scatter(
-        dot_nt(hidden, out_full).astype(jnp.bfloat16), "tensor", scatter_dimension=0, tiled=True
-    ).astype(jnp.float32)
-    output = tokens + branch
-    cot_rows = lax.all_gather(cotangent.astype(jnp.bfloat16), "tensor", axis=0, tiled=True)
-    z_back, x_back, dt_back, out_back = (z_full, x_full, dt_full, out_full)
-    d_hidden = jnp.dot(cot_rows, out_back, preferred_element_type=jnp.float32)
-    g_w_out = lax.psum_scatter(dot_tn(cot_rows, hidden), "dp", scatter_dimension=0, tiled=True)
+    d_hidden = jnp.dot(cot_rows, out_full, preferred_element_type=jnp.float32)
+    g_w_out_part = dot_tn(cot_rows, hidden).astype(jnp.bfloat16)
+    branch_part = dot_nt(hidden, out_full).astype(jnp.bfloat16)
     d_unit = d_hidden * norm_w[None, :] * token_mask[:, None]
     g_norm_w = jnp.sum(d_hidden * unit_g * token_mask[:, None], axis=0)
     inner_sum = lax.psum(jnp.sum(d_unit * unit_g, axis=1), "tensor")
@@ -200,39 +234,68 @@
     sigmoid_gate = jax.nn.sigmoid(gate_pre)
     d_y = d_gated * gate_pre * sigmoid_gate
     d_gate = d_gated * y_local * sigmoid_gate * (1.0 + gate_pre * (1.0 - sigmoid_gate))
+    gate_g = d_gate.astype(jnp.bfloat16)
+    g_w_z_part = dot_tn(normed, gate_g).astype(jnp.bfloat16)
+    d_y, g_w_out_part, branch_part, g_w_z_part = lax.optimization_barrier(
+        (d_y, g_w_out_part, branch_part, g_w_z_part)
+    )
+    g_w_out = scatter_dp(g_w_out_part)
+    g_w_z = scatter_dp(g_w_z_part)
+    branch = lax.psum_scatter(branch_part, "tensor", scatter_dimension=0, tiled=True)
+    output = tokens + branch.astype(jnp.float32)
     d_xp, d_bc, d_dt, g_cxw, g_cxb, g_cbw, g_cbb, g_alog, g_skip, g_bias = scan_back(d_y)
-    gate_g = d_gate.astype(jnp.bfloat16)
     x_g = d_xp.astype(jnp.bfloat16)
     dt_g = d_dt.astype(jnp.bfloat16)
     bc_g = d_bc.astype(jnp.bfloat16)
-    joined = jnp.concatenate([gate_g, x_g, dt_g], axis=1)
-    in_grads = lax.psum_scatter(dot_tn(normed, joined), "dp", scatter_dimension=0, tiled=True)
-    width_local = w_z.shape[1]
-    g_w_z = in_grads[:, :width_local]
-    g_w_x = in_grads[:, width_local : 2 * width_local]
-    g_w_dt = in_grads[:, 2 * width_local :]
-    g_w_bc_part = dot_tn(normed, bc_g)
-    summed = dot_nt(gate_g, z_back) + dot_nt(x_g, x_back)
+    d_normed_part = dot_nt(gate_g, z_full) + dot_nt(x_g, x_full)
+    d_normed_part = d_normed_part + dot_nt(dt_g, dt_full) + dot_nt(bc_g, bc_weight)
+    joined = jnp.concatenate([x_g, bc_g, dt_g], axis=1)
+    in_grads = scatter_dp(dot_tn(normed, joined))
+    g_w_x = in_grads[:, :width_local]
+    g_bc_rows = in_grads[:, width_local : width_local + bc_width]
+    g_w_dt = in_grads[:, width_local + bc_width :]
     d_normed = lax.psum_scatter(
-        summed + dot_nt(dt_g, dt_back) + dot_nt(bc_g, bc_weight),
-        "tensor",
-        scatter_dimension=0,
-        tiled=True,
-    )
-    g_gain_part = jnp.sum(d_normed * unit_rows, axis=0)
+        d_normed_part.astype(jnp.bfloat16), "tensor", scatter_dimension=0, tiled=True
+    ).astype(jnp.float32)
     d_unit_r = d_normed * gain_full[None, :]
     d_tokens = cotangent + inv_rms * (
         d_unit_r - unit_rows * jnp.mean(d_unit_r * unit_rows, axis=1, keepdims=True)
     )
-    g_w_bc, g_gain, g_conv_bcw, g_conv_bcb = (
-        lax.psum_scatter(g_w_bc_part, ("dp", "tensor"), scatter_dimension=0, tiled=True),
-        lax.psum_scatter(g_gain_part, ("dp", "tensor"), scatter_dimension=0, tiled=True),
-        lax.psum_scatter(g_cbw, ("dp", "tensor"), scatter_dimension=0, tiled=True),
-        lax.psum_scatter(g_cbb, ("dp", "tensor"), scatter_dimension=0, tiled=True),
-    )
-    g_cxw, g_cxb, g_alog, g_skip, g_bias, g_norm_w = lax.psum(
-        (g_cxw, g_cxb, g_alog, g_skip, g_bias, g_norm_w), "dp"
-    )
+
+    group_parts = (g_cxw, g_cxb, g_alog, g_skip, g_bias, g_norm_w, g_cbw, g_cbb)
+    flat = lax.psum(jnp.concatenate([part.reshape(-1) for part in group_parts]), "dp")
+    pieces = []
+    offset = 0
+    for part in group_parts:
+        pieces.append(flat[offset : offset + part.size].reshape(part.shape))
+        offset += part.size
+    g_cxw, g_cxb, g_alog, g_skip, g_bias, g_norm_w, g_cbw, g_cbb = pieces
+
+    dp_index = lax.axis_index("dp")
+    bc_here = lax.dynamic_slice_in_dim(bc_weight, dp_index * weight_rows, weight_rows, 0)
+    gain_rows = (
+        jnp.sum(g_w_z * w_z.astype(jnp.float32), axis=1)
+        + jnp.sum(g_w_x * w_x.astype(jnp.float32), axis=1)
+        + jnp.sum(g_w_dt * w_dt.astype(jnp.float32), axis=1)
+        + jnp.sum(g_bc_rows * bc_here.astype(jnp.float32), axis=1)
+    )
+    conv_here = tensor_size * conv_len
+    cbw_here = lax.dynamic_slice_in_dim(g_cbw, dp_index * conv_here, conv_here, 0)
+    cbb_here = lax.dynamic_slice_in_dim(g_cbb, dp_index * conv_here, conv_here, 0)
+    g_w_bc = tensor_scatter_sum(g_bc_rows.reshape(tensor_size, bc_rows, bc_width))
+    shared = tensor_scatter_sum(
+        jnp.concatenate(
+            [
+                gain_rows.reshape(tensor_size, gain_len),
+                cbw_here.reshape(tensor_size, conv_len * taps),
+                cbb_here.reshape(tensor_size, conv_len),
+            ],
+            axis=1,
+        )
+    )
+    g_gain = shared[:gain_len] / norm_gain
+    g_conv_bcw = shared[gain_len : gain_len + conv_len * taps].reshape(conv_len, taps)
+    g_conv_bcb = shared[gain_len + conv_len * taps :]
     return (
         output,
         d_tokens,

time: 883 us -> 579 us (0.66)
  blocking collectives: 304 us -> 113 us
  waiting for transfers between devices: 266 us -> 167 us
  matrix products: 166 us -> 130 us
  local copies, waits for them, and re-layouts: 46.8 us -> 63.7 us
    all_gather x3 -> x0, blocking collectives: 156 us -> none  [the longest x1 70.3 us: per_device(): lax.all_gather(w_bc.astype(jnp.float32), ('dp', 'tensor'), axis=0, tiled=...]
    reduce_scatter x4, waiting for transfers between devices: 191 us -> 60.7 us  [the longest x1 32.5 us: per_device(): lax.psum_scatter(branch_part, 'tensor', scatter_dimension=0, tiled=True)]
    all_gather x5 -> x4, waiting for transfers between devices: 0.04 us -> 37.8 us  [the longest x1 29.4 us: per_device(): lax.all_gather(jnp.concatenate([normed_own, bc_extra], axis=0), 'tensor',...]
    unnamed x2 -> x1, blocking collectives: 80.5 us -> 43.6 us
    dot_general x9, matrix products: 88.3 us -> 62.7 us  [the longest x3 45.3 us: scan_heads(): y_local = jnp.einsum('sijh,sjhp->sihp', mixing, inputs, precision=HIGH_PREC)]
    reshape x0 -> x18, local copies, waits for them, and re-layouts: none -> 13.3 us  [the longest x4 6.37 us: scan_heads(): state_in = bc_conv[:, :STATE].reshape(slot_count, BLOCK, STATE)]
    reduce_sum x2 -> x1, other arithmetic: 11.8 us -> 0.12 us  [scan_heads(): output = y_local + y_state + inputs * d_skip[None, None, :, None]]
    convert_element_type x0 -> x3, other arithmetic: none -> 10.4 us  [the longest x1 8.72 us: per_device(): gate_g = d_gate.astype(jnp.bfloat16)]
  transfers between devices with their start and end apart: 10 -> 11, of which waited for: 3 -> 8; matrix products, arithmetic and copies ran while one was open for 14% -> 28% of each run, Pallas kernels for 0% -> 0%
where the time goes in v1:
time: 579 us; the launch traced here: 574 us
  waiting for transfers between devices  167 us (29%)
  matrix products  130 us (22%)
  blocking collectives  113 us (20%)
  other arithmetic  80.7 us (14%)
  local copies, waits for them, and re-layouts  63.7 us (11%)
  between operations  16.4 us (3%)
    unnamed x10, waiting for transfers between devices  67 us
    psum x1, blocking collectives, per_device(): lax.psum(jnp.concatenate([part.reshape(-1) for part in group_parts]), 'dp')  59.2 us
    dot_general x3, matrix products, scan_heads(): y_local = jnp.einsum('sijh,sjhp->sihp', mixing, inputs, precision=HIGH_PREC)  45.3 us
    unnamed x1, blocking collectives  43.6 us
    reduce_scatter x1, waiting for transfers between devices, per_device(): lax.psum_scatter(branch_part, 'tensor', scatter_dimension=0, tiled=True)  32.5 us
    all_gather x1, waiting for transfers between devices, per_device(): lax.all_gather(jnp.concatenate([normed_own, bc_extra], axis=0), 'tensor',...  29.4 us
    reduce_scatter x1, waiting for transfers between devices, per_device(): lax.psum_scatter(d_normed_part.astype(jnp.bfloat16), 'tensor', scatter_di...  24.5 us
    dot_general x5, matrix products, dot_nt(): lax.dot_general(left, right, (((1,), (1,)), ((), ())), preferred_element_...  19.9 us
  transfers between devices with their start and end apart: 11, of which 8 were waited for; matrix products, arithmetic and copies ran while one was open for 28% of the time, Pallas kernels for 0%

profile of v1, /device:TPU:0, one launch (start us, length us, event | category | flops | bytes accessed | tf_op | source)
XLA Modules:
  0.0 574.2 jit_solution(7533726888070533971)
XLA Ops:
  8.9 1.7 pad_maximum_fusion.2
  12.4 43.6 %all-reduce.29 = f32[2304]{0:T(1024)S(1)} all-reduce(f32[2304]{0:T(1024)S(1)} %maximum_dynamic-update-slice_fusion), channel_id=2, replica_groups=mesh['dp'=16,'tensor'=2] {'dp','tensor'}, use_global_device_ids=true, to_apply=%add.29 | all-reduce | flops 2304 | bytes 18432
  56.2 1.9 multiply_reduce_fusion.12
  59.0 8.4 %all-gather.7.cloned.1.call-done = bf16[1024,2192]{1,0:T(8,128)(2,1)} async-done(((bf16[64,2192]{1,0:T(8,128)(2,1)}), bf16[1024,2192]{1,0:T(8,128)(2,1)}) %all-gather.7.cloned.1.call-update) | async-done | bytes 4489232 | tf_op jit(solution)/shard_map/all_gather | solution.py:150
  70.0 2.7 convert_element_type.82
  78.0 29.4 %all-gather.13.cloned.1.call-done = bf16[1280,1024]{1,0:T(8,128)(2,1)} async-done(((bf16[640,1024]{1,0:T(8,128)(2,1)}), bf16[1280,1024]{1,0:T(8,128)(2,1)}) %all-gather.13.cloned.1.call-update) | async-done | bytes 2621456 | tf_op jit(solution)/shard_map/all_gather | solution.py:171
  107.4 1.8 slice.243
  109.1 1.5 slice.249
  112.3 1.8 fusion.167
  114.2 2.2 fusion.94
  116.4 6.2 %fusion.73 = f32[1024,1024]{0,1:T(8,128)} fusion(bf16[1024,1024]{1,0:T(8,128)(2,1)S(1)} %bitcast.247, bf16[1024,2192]{1,0:T(8,128)(2,1)} %all-gather.7.cloned.1.call-done), kind=kOutput, calls=%fused_computation.110 | convolution fusion | flops 2147483648 | bytes 8388608 | tf_op jit(solution)/shard_map/dot_general | solution.py:189
  123.6 2.1 reshape.416
  125.7 2.0 copy.301
  127.8 2.1 reshape.417
  129.8 2.0 copy.302
  131.9 2.1 copy.341
  134.0 12.8 %fusion.30 = (f32[1024,1024]{0,1:T(8,128)}, f32[1024,1024]{0,1:T(8,128)}) fusion(f32[1024]{0:T(1024)S(1)} %bitcast.287, f32[1024,1024]{0,1:T(8,128)} %fusion.73, f32[1024]{0:T(1024)S(1)} %get-tuple-element.216, f32[1024]{0:T(1024)S(1)} %bitcast.281, f32[1024]{0:T(1024)S(1)} %get-tuple-element.217, f32[1023,1024]{0,1:T(8,128)} %bitcast.234, ...), kind=kLoop, calls=%fused_computation.59 | loop fusion | flops 16777216 | bytes 25178112 | tf_op jit(solution)/shard_map/jvp(jit(silu))/mul | solution.py:31
  146.8 5.6 reshape.412
  152.4 1.6 broadcast_multiply_fusion
  155.6 4.6 fusion.75
  160.3 2.3 fusion.95
  163.8 1.9 fusion.169
  165.7 2.0 copy-done.13
  167.7 11.1 %fusion.29 = f32[4,256,16,64]{1,3,2,0:T(8,128)S(1)} fusion(f32[4,256,16,64]{1,3,2,0:T(8,128)S(1)} %bitcast.256, f32[4,256,16,64]{1,0,3,2:T(4,128)S(1)} %copy-done.4, f32[4,256,16]{1,2,0:T(8,128)S(1)} %bitcast.278, f32[4,256,16]{1,2,0:T(8,128)S(1)} %convolution_bitcast_fusion.1, f32[4,256,256]{2,1,0:T(8,128)S(1)} %fusion.168, ...), kind=kOutput, calls=%fused_computation.38 | convolution fusion | flops 1631584256 | bytes 13893696 | tf_op jit(solution)/shard_map/jvp(sijh,sjhp->sihp)/dot_general | solution.py:71
  178.7 2.8 copy.311
  182.6 9.7 %multiply_reduce_fusion.10 = (f32[1024]{0:T(1024)S(1)}, f32[1024,1024]{0,1:T(8,128)}, f32[1024,1024]{0,1:T(8,128)}) fusion(f32[1024,1024]{0,1:T(8,128)S(1)} %bitcast.252, bf16[1024,1024]{1,0:T(8,128)(2,1)S(1)} %bitcast.249, bf16[1024,2192]{1,0:T(8,128)(2,1)} %all-gather.7.cloned.1.call-done), kind=kOutput, calls=%fused_computation.55 | convolution fusion | flops 2154822656 | bytes 16781312 | tf_op jit(solution)/shard_map/dot_general | solution.py:188
  192.3 5.1 psum.21
  197.4 6.7 %convolution_convert_fusion.3 = bf16[1024,1024]{1,0:T(8,128)(2,1)} fusion(bf16[1024,1024]{1,0:T(8,128)(2,1)} %all-gather.9.cloned.1.call-done, f32[1024,1024]{0,1:T(8,128)} %get-tuple-element.181, f32[1024]{0:T(1024)S(1)} %fusion.139, f32[1024]{0:T(1024)S(1)} %copy-done.85, f32[1024]{0:T(1024)S(1)} %add_rsqrt_fusion), kind=kOutput, calls=%fused_computation.103 | convolution fusion | flops 2152726528 | bytes 8400896 | tf_op jit(solution)/shard_map/dot_general | solution.py:101
  204.2 9.3 %multiply_reduce_fusion.2 = (f32[1024]{0:T(1024)}, f32[1024]{0:T(1024)S(1)}, f32[1024,1024]{0,1:T(8,128)}) fusion(f32[1024,1024]{0,1:T(8,128)} %get-tuple-element.181, f32[1024]{0:T(1024)S(1)} %fusion.139, f32[1024]{0:T(1024)S(1)} %add_rsqrt_fusion, f32[1024]{0:T(1024)S(1)} %copy-done.85, bf16[1024,1024]{1,0:T(8,128)(2,1)} %all-gather.9.cloned.1.call-done, ...), kind=kOutput, calls=%fused_computation.40 | convolution fusion | flops 2155870208 | bytes 12603392 | tf_op jit(solution)/shard_map/dot_general | solution.py:227
  213.4 4.9 psum.22
  218.3 8.7 %multiply_convert_fusion = (bf16[1024,1024]{0,1:T(8,128)(2,1)S(1)}, f32[1024,1024]{0,1:T(8,128)}) fusion(f32[1024,1024]{0,1:T(8,128)} %get-tuple-element.226, f32[1024,1024]{0,1:T(8,128)} %bitcast.253, f32[1024]{0:T(1024)S(1)} %psum.22, f32[1024,1024]{0,1:T(8,128)} %get-tuple-element.181, f32[1024]{0:T(1024)S(1)} %fusion.139, ...), kind=kLoop, calls=%fused_computation.49 | loop fusion | flops 19922944 | bytes 23085056 | tf_op jit(solution)/shard_map/convert_element_type | solution.py:237
  228.4 3.7 convolution_convert_fusion.1
  232.1 6.8 %convolution_convert_fusion.2 = bf16[1024,1024]{1,0:T(8,128)(2,1)} fusion(bf16[1024,1024]{1,0:T(8,128)(2,1)} %all-gather.11.cloned.1.call-done, f32[1024,1024]{0,1:T(8,128)} %get-tuple-element.181, f32[1024]{0:T(1024)S(1)} %fusion.139, f32[1024]{0:T(1024)S(1)} %copy-done.85, f32[1024]{0:T(1024)S(1)} %add_rsqrt_fusion), kind=kOutput, calls=%fused_computation.102 | convolution fusion | flops 2152726528 | bytes 8400896 | tf_op jit(solution)/shard_map/dot_general | solution.py:95
  238.9 5.7 reshape.421
  244.7 23.8 %fusion.8 = (f32[4,256,16]{1,2,0:T(8,128)}, f32[4,256,16]{1,2,0:T(8,128)}, f32[4,256,16]{1,2,0:T(8,128)}, f32[4,256,256]{2,1,0:T(8,128)S(1)}) fusion(f32[4,256,16]{1,2,0:T(8,128)S(1)} %bitcast.279, f32[4,256,16]{1,2,0:T(8,128)S(1)} %convolution_bitcast_fusion.1, f32[4,256,256]{2,1,0:T(8,128)} %copy-done.36, pred[256,256]{1,0:T(8,128)(4,1)S(1)} %copy-done.47, ...), kind=kOutput, calls=%fused_computation.11 | convolution fusion | flops 1664827392 | bytes 10878976 | tf_op jit(solution)/shard_map/transpose(jvp(sijh,sjhp->sihp))/dot_general | solution.py:71
  268.5 3.6 fusion.86
  272.1 2.3 fusion.78
  274.5 2.8 fusion.100
  277.3 1.6 add_multiply_fusion
  278.9 3.5 fusion.81
  282.5 1.8 fusion.61
  284.3 10.4 %bitcast_add_fusion = f32[4,256,16,64]{1,3,2,0:T(8,128)} fusion(f32[4,256,16,64]{1,3,2,0:T(8,128)S(1)} %fusion.61, f32[4,256,16,64]{1,0,3,2:T(4,128)S(1)} %copy-done.6, f32[4,256,16]{1,2,0:T(8,128)S(1)} %bitcast.280, f32[4,256,16]{1,2,0:T(8,128)S(1)} %convolution_bitcast_fusion.1, f32[4,256,256]{2,1,0:T(8,128)S(1)} %copy-done.37, ...), kind=kOutput, calls=%fused_computation.33 | convolution fusion | flops 1631584256 | bytes 13893696 | tf_op jit(solution)/shard_map/transpose(jvp(sijh,sjhp->sihp))/dot_general | solution.py:71
  294.8 3.7 multiply_reduce_fusion.1
  301.7 5.0 copy.318
  306.7 2.9 copy.371
  309.8 5.1 multiply_reduce_fusion.8
  319.0 9.6 %fusion.152 = (f32[1024]{0:T(1024)S(1)}, f32[1024]{0:T(1024)S(1)}, f32[1024]{0:T(1024)S(1)}, f32[1024]{0:T(1024)S(1)}, f32[1024]{0:T(1024)S(1)}, /*index=5*/f32[1024,1024]{0,1:T(8,128)}, f32[1024]{0:T(1024)S(1)}) fusion(f32[1024]{0:T(1024)S(1)} %get-tuple-element.215, f32[1021,1024]{0,1:T(8,128)S(1)} %bitcast.239, f32[1024]{0:T(1024)S(1)} %get-tuple-element.218, ...), kind=kLoop, calls=%fused_computation.261 | loop fusion | flops 26208256 | bytes 33570816 | tf_op jit(solution)/shard_map/transpose(jvp())/reduce_sum | solution.py:26
  331.4 1.4 fusion.23
  334.3 1.4 fusion.25
  338.3 4.8 convolution_convert_fusion
  343.4 1.9 fusion.170
  345.3 4.2 fusion.67
  349.5 4.0 fusion.71
  353.5 3.0 add_convert_fusion
  358.9 59.2 %psum.23 = f32[7472]{0:T(1024)S(1)} all-reduce(f32[7472]{0:T(1024)S(1)} %concatenate.50), channel_id=1, replica_groups=mesh['dp'=16,'tensor'=2] {'dp'}, use_global_device_ids=true, to_apply=%region_38.39 | all-reduce | flops 7472 | bytes 59776 | tf_op jit(solution)/shard_map/psum | solution.py:266
  421.2 1.6 convert_element_type.105
  422.9 3.8 reduce-scatter.12.cloned.1.call-done
  426.7 1.7 multiply_reduce_fusion.19
  428.4 66.2 %reduce-scatter.16.cloned.1.call-done = bf16[64,1296]{1,0:T(8,128)(2,1)} async-done(((bf16[1024,1296]{1,0:T(8,128)(2,1)}), bf16[64,1296]{1,0:T(8,128)(2,1)}) %reduce-scatter.16.cloned.1.call-update) | async-done | bytes 165904
  496.8 1.5 collective-permute-start
  503.9 24.5 %reduce-scatter.10.cloned.1.call-done = bf16[512,1024]{1,0:T(8,128)(2,1)} async-done(((bf16[1024,1024]{1,0:T(8,128)(2,1)}), bf16[512,1024]{1,0:T(8,128)(2,1)}) %reduce-scatter.10.cloned.1.call-update) | async-done | bytes 1048592 | tf_op jit(solution)/shard_map/reduce_scatter | solution.py:257
  528.4 1.7 multiply_reduce_fusion.11
  530.1 32.5 %reduce-scatter.8.cloned.1.call-done = bf16[512,1024]{1,0:T(8,128)(2,1)} async-done(((bf16[1024,1024]{1,0:T(8,128)(2,1)}), bf16[512,1024]{1,0:T(8,128)(2,1)}) %reduce-scatter.8.cloned.1.call-update) | async-done | bytes 1048592 | tf_op jit(solution)/shard_map/reduce_scatter | solution.py:244
  562.6 4.9 multiply_add_fusion.1
  (333 shorter events, 46.5 us)
Async XLA Ops:
  7.2 65.7 %copy-start = (s32[4]{0:T(128)S(1)}, s32[4]{0:T(128)}, u32[]{:S(2)}) copy-start(s32[4]{0:T(128)} %param.34) | copy-start | bytes 52
  7.2 51.5 %copy-start.8 = (f32[512,1024]{1,0:T(8,128)S(1)}, f32[512,1024]{1,0:T(8,128)}, u32[]{:S(2)}) copy-start(f32[512,1024]{1,0:T(8,128)} %param.18) | copy-start | bytes 6291460
  7.2 60.1 %all-gather.7.cloned.1.call-start = ((), (), s32[]{:S(2)}) async-start(), calls=%async_computation.5 | async-start | bytes 5013504 | tf_op jit(solution)/shard_map/all_gather | solution.py:150
  10.6 96.7 %all-gather.13.cloned.1.call-start = ((), (), s32[]{:S(2)}) async-start(), calls=%async_computation.12 | async-start | bytes 3932160 | tf_op jit(solution)/shard_map/all_gather | solution.py:171
  56.2 13.4 %copy-start.40 = (f32[1024]{0:T(1024)}, f32[1024]{0:T(1024)S(1)}, u32[]{:S(2)}) copy-start(f32[1024]{0:T(1024)S(1)} %mul.746) | copy-start | bytes 12292
  58.1 11.6 %copy-start.92 = (s32[4]{0:T(128)S(1)}, s32[4]{0:T(128)}, u32[]{:S(2)}) copy-start(s32[4]{0:T(128)} %param.33) | copy-start | bytes 52
  68.3 9.5 %copy-start.98 = (f32[16]{0:T(128)S(1)}, f32[16]{0:T(128)}, u32[]{:S(2)}) copy-start(f32[16]{0:T(128)} %param.29) | copy-start | bytes 196
  68.3 9.6 %copy-start.68 = (f32[1024,4]{0,1:T(4,128)S(1)}, f32[1024,4]{0,1:T(4,128)}, u32[]{:S(2)}) copy-start(f32[1024,4]{0,1:T(4,128)} %param.25) | copy-start | bytes 49156
  69.6 127.8 %all-gather.9.cloned.1.call-start = ((), (), s32[]{:S(2)}) async-start(), calls=%async_computation.6 | async-start | bytes 3145728 | tf_op jit(solution)/shard_map/all_gather | solution.py:180
  77.8 36.3 %copy-start.72 = (f32[256]{0:T(256)}, f32[256]{0:T(256)S(1)}, u32[]{:S(2)}) copy-start(f32[256]{0:T(256)S(1)} %get-tuple-element.162) | copy-start | bytes 3076
  77.8 36.3 %copy-start.74 = (f32[256]{0:T(256)}, f32[256]{0:T(256)S(1)}, u32[]{:S(2)}) copy-start(f32[256]{0:T(256)S(1)} %get-tuple-element.163) | copy-start | bytes 3076
  77.8 36.3 %copy-start.76 = (f32[256]{0:T(256)}, f32[256]{0:T(256)S(1)}, u32[]{:S(2)}) copy-start(f32[256]{0:T(256)S(1)} %get-tuple-element.164) | copy-start | bytes 3076
  77.8 36.3 %copy-start.78 = (f32[256]{0:T(256)}, f32[256]{0:T(256)S(1)}, u32[]{:S(2)}) copy-start(f32[256]{0:T(256)S(1)} %get-tuple-element.161) | copy-start | bytes 3076
  77.9 74.6 %copy-start.88 = (f32[16]{0:T(128)}, f32[16]{0:T(128)S(1)}, u32[]{:S(2)}) copy-start(f32[16]{0:T(128)S(1)} %exponential_negate_fusion) | copy-start | bytes 196
  77.9 154.2 %copy-start.42 = (f32[1024]{0:T(1024)}, f32[1024]{0:T(1024)S(1)}, u32[]{:S(2)}) copy-start(f32[1024]{0:T(1024)S(1)} %fusion.139) | copy-start | bytes 12292
  77.9 56.0 %copy-start.55 = (f32[1024,1]{0,1:T(1,128)}, f32[1024,1]{0,1:T(1,128)S(1)}, u32[]{:S(2)}) copy-start(f32[1024,1]{0,1:T(1,128)S(1)} %get-tuple-element.212) | copy-start | bytes 12292
  77.9 56.0 %copy-start.57 = (f32[1024,1]{0,1:T(1,128)}, f32[1024,1]{0,1:T(1,128)S(1)}, u32[]{:S(2)}) copy-start(f32[1024,1]{0,1:T(1,128)S(1)} %get-tuple-element.210) | copy-start | bytes 12292
  77.9 56.0 %copy-start.59 = (f32[1024,1]{0,1:T(1,128)}, f32[1024,1]{0,1:T(1,128)S(1)}, u32[]{:S(2)}) copy-start(f32[1024,1]{0,1:T(1,128)S(1)} %get-tuple-element.209) | copy-start | bytes 12292
  78.0 56.0 %copy-start.61 = (f32[1024,1]{0,1:T(1,128)}, f32[1024,1]{0,1:T(1,128)S(1)}, u32[]{:S(2)}) copy-start(f32[1024,1]{0,1:T(1,128)S(1)} %get-tuple-element.211) | copy-start | bytes 12292
  109.1 117.9 %copy-start.10 = (bf16[2,512,1024]{2,1,0:T(8,128)(2,1)}, bf16[2,512,1024]{2,1,0:T(8,128)(2,1)S(1)}, u32[]{:S(2)}) copy-start(bf16[2,512,1024]{2,1,0:T(8,128)(2,1)S(1)} %slice.243) | copy-start | bytes 6291460
  111.8 92.4 %all-gather.11.cloned.1.call-start = ((), (), s32[]{:S(2)}) async-start(), calls=%async_computation.7 | async-start | bytes 2228224 | tf_op jit(solution)/shard_map/all_gather | solution.py:181
  122.6 11.4 %copy-start.87 = (f32[1024]{0:T(1024)S(1)}, f32[1024]{0:T(1024)}, u32[]{:S(2)}) copy-start(f32[1024]{0:T(1024)} %param.26) | copy-start | bytes 12292
  146.8 5.6 copy-start.93
  155.1 7.5 %copy-start.70 = (f32[16]{0:T(128)}, f32[16]{0:T(128)S(1)}, u32[]{:S(2)}) copy-start(f32[16]{0:T(128)S(1)} %get-tuple-element.167) | copy-start | bytes 196
  155.1 7.5 %copy-start.80 = (f32[16]{0:T(128)}, f32[16]{0:T(128)S(1)}, u32[]{:S(2)}) copy-start(f32[16]{0:T(128)S(1)} %get-tuple-element.166) | copy-start | bytes 196
  155.1 7.5 %copy-start.83 = (f32[16]{0:T(128)}, f32[16]{0:T(128)S(1)}, u32[]{:S(2)}) copy-start(f32[16]{0:T(128)S(1)} %get-tuple-element.168) | copy-start | bytes 196
  155.2 7.4 %copy-start.63 = (f32[4,16]{1,0:T(4,128)}, f32[4,16]{1,0:T(4,128)S(1)}, u32[]{:S(2)}) copy-start(f32[4,16]{1,0:T(4,128)S(1)} %slice_reduce_fusion.4) | copy-start | bytes 772
  155.3 265.9 %reduce-scatter.14.cloned.1.call-start = ((), (), s32[]{:S(2)}) async-start(), calls=%async_computation.11 | async-start | bytes 2228224 | tf_op jit(solution)/shard_map/reduce_scatter | solution.py:118
  155.6 7.0 %copy-start.17 = (f32[4,256,128]{2,1,0:T(8,128)S(1)}, f32[4,256,128]{2,1,0:T(8,128)}, u32[]{:S(2)}) copy-start(f32[4,256,128]{2,1,0:T(8,128)} %copy.301) | copy-start | bytes 1572868
  155.6 7.0 %copy-start.20 = (f32[4,256,128]{2,1,0:T(8,128)S(1)}, f32[4,256,128]{2,1,0:T(8,128)}, u32[]{:S(2)}) copy-start(f32[4,256,128]{2,1,0:T(8,128)} %copy.302) | copy-start | bytes 1572868
  182.5 9.8 %copy-start.12 = (f32[128,8,4,256]{3,1,2,0:T(8,128)}, f32[128,8,4,256]{3,1,2,0:T(8,128)S(1)}, u32[]{:S(2)}) copy-start(f32[128,8,4,256]{3,1,2,0:T(8,128)S(1)} %copy.370) | copy-start | bytes 12582916
  182.6 14.9 %copy-start.85 = (f32[1024]{0:T(1024)S(1)}, f32[1024]{0:T(1024)}, u32[]{:S(2)}) copy-start(f32[1024]{0:T(1024)} %param.32) | copy-start | bytes 12292
  238.9 5.7 copy-start.47
  238.9 5.7 copy-start.49
  244.6 23.9 %copy-start.6 = (f32[4,256,16,64]{1,0,3,2:T(4,128)S(1)}, f32[4,256,16,64]{1,0,3,2:T(4,128)}, u32[]{:S(2)}) copy-start(f32[4,256,16,64]{1,0,3,2:T(4,128)} %reshape.421) | copy-start | bytes 12582916
  244.6 23.9 %copy-start.31 = (f32[1,16,128,64]{2,3,1,0:T(8,128)S(1)}, f32[1,16,128,64]{2,3,1,0:T(8,128)}, u32[]{:S(2)}) copy-start(f32[1,16,128,64]{2,3,1,0:T(8,128)} %copy-done.30) | copy-start | bytes 1572868
  244.6 23.8 %copy-start.33 = (f32[1,16,128,64]{2,3,1,0:T(8,128)S(1)}, f32[1,16,128,64]{2,3,1,0:T(8,128)}, u32[]{:S(2)}) copy-start(f32[1,16,128,64]{2,3,1,0:T(8,128)} %copy-done.32) | copy-start | bytes 1572868
  244.7 23.8 %copy-start.35 = (f32[1,16,128,64]{2,3,1,0:T(8,128)S(1)}, f32[1,16,128,64]{2,3,1,0:T(8,128)}, u32[]{:S(2)}) copy-start(f32[1,16,128,64]{2,3,1,0:T(8,128)} %copy-done.34) | copy-start | bytes 1572868
  244.7 23.8 %copy-start.95 = (f32[4]{0:T(128)S(1)}, f32[4]{0:T(128)}, u32[]{:S(2)}) copy-start(f32[4]{0:T(128)} %pad.104.clone) | copy-start | bytes 52
  277.3 5.1 copy-start.22
  300.3 126.4 %reduce-scatter.12.cloned.1.call-start = ((), (), s32[]{:S(2)}) async-start(), calls=%async_computation.10 | async-start | bytes 2228224 | tf_op jit(solution)/shard_map/reduce_scatter | solution.py:118
  309.8 5.2 copy-start.44
  309.8 5.2 copy-start.45
  309.8 5.2 copy-start.65
  309.8 5.5 copy-start.24
  309.8 7.7 %copy-start.14 = (f32[128,8,4,256]{3,1,2,0:T(8,128)S(1)}, f32[128,8,4,256]{3,1,2,0:T(8,128)}, u32[]{:S(2)}) copy-start(f32[128,8,4,256]{3,1,2,0:T(8,128)} %copy.371) | copy-start | bytes 12582916
  319.0 10.1 %copy-start.43 = (f32[1024]{0:T(1024)S(1)}, f32[1024]{0:T(1024)}, u32[]{:S(2)}) copy-start(f32[1024]{0:T(1024)} %copy-done.42) | copy-start | bytes 12292
  319.0 10.1 %copy-start.89 = (f32[16]{0:T(128)S(1)}, f32[16]{0:T(128)}, u32[]{:S(2)}) copy-start(f32[16]{0:T(128)} %copy-done.88) | copy-start | bytes 196
  319.0 10.3 %copy-start.52 = (f32[1023]{0:T(1024)S(1)}, f32[1023]{0:T(1024)}, u32[]{:S(2)}) copy-start(f32[1023]{0:T(1024)} %slice.269) | copy-start | bytes 12280
  319.0 10.3 %copy-start.75 = (f32[256]{0:T(256)S(1)}, f32[256]{0:T(256)}, u32[]{:S(2)}) copy-start(f32[256]{0:T(256)} %copy-done.74) | copy-start | bytes 3076
  328.6 166.0 %reduce-scatter.16.cloned.1.call-start = ((), (), s32[]{:S(2)}) async-start(), calls=%async_computation.13 | async-start | bytes 3063808
  330.0 7.0 %copy-start.29 = (bf16[1024,256]{0,1:T(8,128)(2,1)}, bf16[1024,256]{0,1:T(8,128)(2,1)S(1)}, u32[]{:S(2)}) copy-start(bf16[1024,256]{0,1:T(8,128)(2,1)S(1)} %add_convert_fusion.2) | copy-start | bytes 1572868
  338.3 5.1 copy-start.19
  343.1 185.2 %reduce-scatter.10.cloned.1.call-start = ((), (), s32[]{:S(2)}) async-start(), calls=%async_computation.9 | async-start | bytes 3145728 | tf_op jit(solution)/shard_map/reduce_scatter | solution.py:257
  356.6 70.1 %copy-start.39 = (bf16[64,1024]{1,0:T(8,128)(2,1)S(1)}, bf16[64,1024]{1,0:T(8,128)(2,1)}, u32[]{:S(2)}) copy-start(bf16[64,1024]{1,0:T(8,128)(2,1)} %param.20) | copy-start | bytes 393220
  356.6 139.4 %copy-start.69 = (bf16[64,16]{0,1:T(8,128)(2,1)S(1)}, bf16[64,16]{0,1:T(8,128)(2,1)}, u32[]{:S(2)}) copy-start(bf16[64,16]{0,1:T(8,128)(2,1)} %param.22) | copy-start | bytes 6148
  356.6 206.0 %reduce-scatter.8.cloned.1.call-start = ((), (), s32[]{:S(2)}) async-start(), calls=%async_computation.8 | async-start | bytes 3145728 | tf_op jit(solution)/shard_map/reduce_scatter | solution.py:244
  358.0 142.4 %copy-start.90 = (f32[32]{0:T(128)S(1)}, f32[32]{0:T(128)}, u32[]{:S(2)}) copy-start(f32[32]{0:T(128)} %param.19) | copy-start | bytes 388
  358.1 170.3 %copy-start.9 = (f32[512,1024]{1,0:T(8,128)S(1)}, f32[512,1024]{1,0:T(8,128)}, u32[]{:S(2)}) copy-start(f32[512,1024]{1,0:T(8,128)} %param.18) | copy-start | bytes 6291460
  358.1 170.3 %copy-start.41 = (f32[1024]{0:T(1024)S(1)}, f32[1024]{0:T(1024)}, u32[]{:S(2)}) copy-start(f32[1024]{0:T(1024)} %copy-done.40) | copy-start | bytes 12292
  358.1 170.3 %copy-start.67 = (f32[512]{0:T(512)S(1)}, f32[512]{0:T(512)}, u32[]{:S(2)}) copy-start(f32[512]{0:T(512)} %copy-done.66) | copy-start | bytes 6148
  496.8 3.6 collective-permute-start
  499.4 3.9 collective-permute-start.1
  530.1 37.4 %copy-start.1 = (s32[4]{0:T(128)S(1)}, s32[4]{0:T(128)}, u32[]{:S(2)}) copy-start(s32[4]{0:T(128)} %param.34) | copy-start | bytes 52
  (47 other events, 109.0 us)
Sparse Core Ops, SparseCore 0:
  10.9 56.4 all-gather.6
  69.8 37.5 all-gather.12
  111.9 33.0 all-gather.8
  155.5 41.3 all-gather.10
  300.4 61.7 reduce-scatter.13
  365.8 60.8 reduce-scatter.11
  430.4 64.1 reduce-scatter.15
  497.4 30.9 reduce-scatter.9
  530.6 31.9 reduce-scatter.7
